TPU v7x, 256 devices: a whole 4x4x8 slice. The times are simulated.
256 devices in a mesh: gy: 16 (over y, x), gx: 16 (over z, core).
Axes of the slice: x: 4, y: 4, z: 8, core: 2. Of those that a mesh axis runs over, the one named last changes fastest.
Arguments:
- direction: float32 [4, 64, 64, 1024], P(None, 'gx', 'gy'), may hold values from -6 to 6
- solution: float32 [4, 64, 64, 1024], P(None, 'gx', 'gy'), may hold values from -6 to 6
- residual: float32 [4, 64, 64, 1024], P(None, 'gx', 'gy'), may hold values from -6 to 6
- north_coef: float32 [64, 1024], P('gy'), may hold values from 0.12 to 0.25
- east_coef: float32 [64, 1024], P('gy'), may hold values from 0.12 to 0.25
- ocean: int32 [64, 1024], P('gy'), may hold values 0 or 1
- vert_coef: float32 [64, 64, 1024], P(None, 'gy', 'gx'), may hold values from 0.1 to 10
- obs_owner: int32 [16, 16, 512, 1], P('gy', 'gx'), may hold values from 0 to 255; in each aligned block of 512 rows (0 to 511, 512 to 1023, ..., all dimensions but the last counted through in order) at most 4 rows name the same one
- obs_row: int32 [16, 16, 512], P('gy', 'gx'), may hold values from 0 to 2
- obs_col: int32 [16, 16, 512], P('gy', 'gx'), may hold values from 0 to 62
- obs_frac: float32 [16, 16, 2, 512], P('gy', 'gx'), may hold values from 0 to 1
- error_inverse: float32 [16, 16, 256, 256], P('gy', 'gx'), may hold values from -3 to 6, as said below
Outputs:
- solution_next: float32 [4, 64, 64, 1024], P(None, 'gx', 'gy')
- residual_next: float32 [4, 64, 64, 1024], P(None, 'gx', 'gy')
- direction_next: float32 [4, 64, 64, 1024], P(None, 'gx', 'gy')
Inputs may be any that keep to these rules, and one draw needn't show every extreme that they name: `obs_owner`: the observations of one device name each owner at most 4 times, and in every draw some device names some owner exactly 4 times. `error_inverse`: symmetric positive definite for every owner.
All inputs are finite; a program needn't handle non-finite values. No bound on the sum of `ocean` on one device may be relied on, other than what follows from the above.
Results may differ from a plain program's by a relative error of at most 0.000078.
Values sent between devices are 32-bit elements; how exact they have to be, the bound alone decides.
A program may use at most 128 MiB of HBM per device.

v0:
```python
import functools

import jax
import jax.numpy as jnp
from jax import lax
from jax.experimental import pallas as pl
from jax.experimental.pallas import tpu as pltpu
from jax.sharding import PartitionSpec as P

NSTEP = 4
N = 16
F32 = jnp.float32
BF16 = jnp.bfloat16


def split(x):
    hi = x.astype(BF16)
    lo = (x - hi.astype(F32)).astype(BF16)
    return hi, lo


def dot(a, b, dims):
    return lax.dot_general(a, b, (dims, ((), ())), preferred_element_type=F32)


def dot3(a_hi, a_lo, b_hi, b_lo, dims):
    return dot(a_hi, b_hi, dims) + (dot(a_hi, b_lo, dims) + dot(a_lo, b_hi, dims))


def exchange(src, dst, axis, me, send_sem, recv_sem):
    def copy(peer, slot):
        return pltpu.make_async_remote_copy(
            src_ref=src(peer),
            dst_ref=dst(slot),
            send_sem=send_sem.at[peer],
            recv_sem=recv_sem.at[slot],
            device_id={axis: peer},
            device_id_type=pl.DeviceIdType.MESH,
        )

    def each(step):
        def body(d, carry):
            step(lax.rem(me + d, N))
            return carry

        lax.fori_loop(1, N, body, 0)

    def start():
        each(lambda peer: copy(peer, me).start())

    def wait_recv():
        each(lambda peer: copy(peer, peer).wait_recv())

    def wait_send():
        each(lambda peer: copy(peer, peer).wait_send())

    return start, wait_recv, wait_send


def kernel(
    dir_ref,
    res_ref,
    coef_ref,
    vert_ref,
    obs_ref,
    own_ref,
    err_ref,
    image_ref,
    scal_ref,
    ua,
    ub,
    uc,
    hc,
    cf,
    inv_ref,
    fa_ref,
    fb_ref,
    fw,
    c_hi,
    c_lo,
    w_hi,
    w_lo,
    e_hi,
    e_lo,
    xs1,
    xr1,
    sm,
    p_ref,
    r1,
    t2,
    a_ref,
    q_ref,
    b_ref,
    u_ref,
    back,
    sp,
    xs2,
    xr2,
    part,
    gat1,
    part2,
    gat2,
    hs_send,
    hs_recv,
    x_send,
    x_recv,
    o_send,
    o_recv,
    r_send,
    r_recv,
):
    gy = lax.axis_index("gy")
    gx = lax.axis_index("gx")

    barrier = pltpu.get_barrier_semaphore()

    def greet(d, carry):
        pl.semaphore_signal(
            barrier,
            inc=1,
            device_id={"gx": lax.rem(gx + d, N)},
            device_id_type=pl.DeviceIdType.MESH,
        )
        pl.semaphore_signal(
            barrier,
            inc=1,
            device_id={"gy": lax.rem(gy + d, N)},
            device_id_type=pl.DeviceIdType.MESH,
        )
        return carry

    lax.fori_loop(1, N, greet, 0)
    pl.semaphore_wait(barrier, 2 * (N - 1))

    def halo_copy(src, dst, sem, toward):
        return pltpu.make_async_remote_copy(
            src_ref=src,
            dst_ref=dst,
            send_sem=hs_send.at[sem],
            recv_sem=hs_recv.at[sem],
            device_id={"gy": toward},
            device_id_type=pl.DeviceIdType.MESH,
        )

    def halo(src, buf, sem):
        def up():
            return halo_copy(src, buf(0), sem, gy + 1)

        def down():
            return halo_copy(src, buf(2), sem + 1, gy - 1)

        def start():
            @pl.when(gy < N - 1)
            def _():
                up().start()

            @pl.when(gy > 0)
            def _():
                down().start()

        def wait_recv():
            @pl.when(gy > 0)
            def _():
                up().wait_recv()

            @pl.when(gy < N - 1)
            def _():
                down().wait_recv()

        def wait_send():
            @pl.when(gy < N - 1)
            def _():
                up().wait_send()

            @pl.when(gy > 0)
            def _():
                down().wait_send()

        return start, wait_recv, wait_send

    coef_halo = halo(coef_ref, lambda b: hc.at[b], 0)
    first_halo = [
        halo(dir_ref.at[h], lambda b, h=h: ua.at[h, pl.ds(4 * b, 4)], 2 + 2 * h)
        for h in range(2)
    ]
    second_halo = [
        halo(uc.at[h, pl.ds(4, 4)], lambda b, h=h: uc.at[h, pl.ds(4 * b, 4)], 6 + 2 * h)
        for h in range(2)
    ]
    coef_halo[0]()
    first_halo[0][0]()
    first_halo[1][0]()

    @pl.when(gy == 0)
    def _():
        hc[0] = jnp.zeros((3, 4, 1024), F32)
        for h in range(2):
            ua[h, pl.ds(0, 4)] = jnp.zeros((4, 8, 1024), F32)
            uc[h, pl.ds(0, 4)] = jnp.zeros((4, 8, 1024), F32)

    @pl.when(gy == N - 1)
    def _():
        hc[2] = jnp.zeros((3, 4, 1024), F32)
        for h in range(2):
            ua[h, pl.ds(8, 4)] = jnp.zeros((4, 8, 1024), F32)
            uc[h, pl.ds(8, 4)] = jnp.zeros((4, 8, 1024), F32)

    hc[1] = coef_ref[...]
    ua[:, pl.ds(4, 4)] = dir_ref[...]

    def factor_row(i, carry):
        v_prev, up_prev = carry
        v = vert_ref[i]
        diagonal = 1.0 + v + v_prev + v_prev * up_prev
        inverse = 1.0 / diagonal
        ratio = v * inverse
        inv_ref[i] = inverse
        fa_ref[i] = v_prev * inverse
        fb_ref[i] = ratio
        return v, -ratio

    zero_row = jnp.zeros((4, 128), F32)
    lax.fori_loop(0, 64, factor_row, (zero_row, zero_row))

    owner_row = own_ref[0:1, :]
    lane512 = lax.broadcasted_iota(jnp.int32, (64, 512), 1)
    sub512 = lax.broadcasted_iota(jnp.int32, (64, 512), 0)
    cell = lax.broadcasted_iota(jnp.int32, (64, 256), 1)
    cell_row = (cell // 64).astype(F32)
    cell_lon = (cell % 64).astype(F32)

    def obs_group(g, rank):
        rows = pl.ds(pl.multiple_of(64 * g, 64), 64)
        block = obs_ref[rows, :]
        o, r, c = block[:, 0:1], block[:, 1:2], block[:, 2:3]
        fr, fc = block[:, 3:4], block[:, 4:5]
        lat = jnp.where(cell_row == r, 1.0 - fr, jnp.where(cell_row == r + 1.0, fr, 0.0))
        lon = jnp.where(cell_lon == c, 1.0 - fc, jnp.where(cell_lon == c + 1.0, fc, 0.0))
        hi, lo = split(lat * lon)
        c_hi[rows, :] = hi
        c_lo[rows, :] = lo
        same = (o == owner_row) & (sub512 + 64 * g < lane512)
        return rank + jnp.sum(jnp.where(same, 1.0, 0.0), axis=0, keepdims=True)

    rank = lax.fori_loop(0, 8, obs_group, jnp.zeros((1, 512), F32))
    owner_int = owner_row.astype(jnp.int32)
    slot = ((owner_int % N) * N + owner_int // N) * 4 + rank.astype(jnp.int32)

    def slot_group(g, carry):
        base = pl.multiple_of(256 * g, 256)
        sub = lax.broadcasted_iota(jnp.int32, (256, 512), 0) + base
        hot = jnp.where(sub == slot, 1.0, 0.0).astype(BF16)
        rows = pl.ds(base, 256)
        w_hi[rows, :] = dot(hot, c_hi[...], ((1,), (0,))).astype(BF16)
        w_lo[rows, :] = dot(hot, c_lo[...], ((1,), (0,))).astype(BF16)
        return carry

    lax.fori_loop(0, 4, slot_group, 0)
    hi, lo = split(err_ref[...])
    e_hi[...] = hi
    e_lo[...] = lo

    def zero_tile():
        return jnp.zeros((8, 1024), F32)

    def rr_group(i, acc):
        x = res_ref[i // 4, i % 4]
        return acc + x * x

    rr = lax.fori_loop(0, 8, rr_group, zero_tile())

    coef_halo[1]()

    def coef_row(i, q):
        return hc[i // 4, q, i % 4 : i % 4 + 1, :]

    fn_prev = jnp.zeros((1, 1024), F32)
    for i in range(12):
        m = coef_row(i, 2)
        if i < 11:
            fn = coef_row(i, 0) * m * coef_row(i + 1, 2)
        else:
            fn = jnp.zeros((1, 1024), F32)
        fe = coef_row(i, 1) * m * pltpu.roll(m, 1023, 1)
        fw_e = pltpu.roll(fe, 1, 1)
        centre = m - fn - fn_prev - fe - fw_e
        for q, value in enumerate((centre, fn, fe, fw_e)):
            cf[i, q] = jnp.broadcast_to(value, (8, 1024))
        fn_prev = fn

    def stencil(src, h, i):
        u = src[h, i]
        return (
            cf[i, 0] * u
            + cf[i, 1] * src[h, i + 1]
            + cf[i - 1, 1] * src[h, i - 1]
            + cf[i, 2] * pltpu.roll(u, 1023, 1)
            + cf[i, 3] * pltpu.roll(u, 1, 1)
        )

    def lateral(buf, h):
        src, dst = buf, ub
        for step in range(NSTEP - 1):

            def row(i, carry, src=src, dst=dst):
                dst[h, i] = stencil(src, h, i)
                return carry

            lax.fori_loop(1 + step, 11 - step, row, 0)
            src, dst = dst, src
        return src

    low = lax.broadcasted_iota(jnp.int32, (8, 128), 1) < 64

    def swap(a, b):
        return (
            jnp.where(low, a, pltpu.roll(b, 64, 1)),
            jnp.where(low, pltpu.roll(a, 64, 1), b),
        )

    x1 = [
        exchange(
            lambda p, h=h: xs1.at[h, p],
            lambda s, h=h: xr1.at[h, s],
            "gx",
            gx,
            x_send.at[h],
            x_recv.at[h],
        )
        for h in range(2)
    ]
    x2 = [
        exchange(
            lambda p, h=h: xs2.at[h, p],
            lambda s, h=h: xr2.at[h, s],
            "gx",
            gx,
            x_send.at[2 + h],
            x_recv.at[2 + h],
        )
        for h in range(2)
    ]

    for h in range(2):
        first_halo[h][1]()
        src = lateral(ua, h)
        for pair in range(2):
            a = stencil(src, h, 4 + 2 * pair)
            b = stencil(src, h, 5 + 2 * pair)
            for t in range(8):
                lanes = slice(128 * t, 128 * t + 128)
                even, odd = swap(a[:, lanes], b[:, lanes])
                xs1[h, 2 * t, 8 * pair : 8 * pair + 8] = even
                xs1[h, 2 * t + 1, 8 * pair : 8 * pair + 8] = odd
        x1[h][0]()
        xr1[h, gx] = xs1[h, gx]

    def vertical(load, store):
        def forward(j, prev):
            for i in range(8):
                k = 8 * j + i
                prev = load(j, i) * inv_ref[k] + fa_ref[k] * prev
                fw[k] = prev
            return prev

        lax.fori_loop(0, 8, forward, zero_row)

        def backward(k, prev):
            j = 7 - k
            for i in range(7, -1, -1):
                prev = fw[8 * j + i] + fb_ref[8 * j + i] * prev
                store(j, i, prev)
            return prev

        lax.fori_loop(0, 8, backward, zero_row)

    def obs_exchange(src, dst, axis, me, k):
        return [
            exchange(
                lambda p, h=h: src(h, p),
                lambda s, h=h: dst(h, s),
                axis,
                me,
                o_send.at[2 * k + h],
                o_recv.at[2 * k + h],
            )
            for h in range(2)
        ]

    o1 = obs_exchange(lambda h, p: p_ref.at[h, p], lambda h, s: r1.at[h, s], "gx", gx, 0)
    o2 = obs_exchange(lambda h, p: t2.at[h, p // 2, p % 2], lambda h, s: a_ref.at[h, s], "gy", gy, 1)
    o3 = obs_exchange(lambda h, p: q_ref.at[h, p], lambda h, s: b_ref.at[h, s], "gy", gy, 2)
    o4 = obs_exchange(lambda h, p: u_ref.at[h, p // 2, p % 2], lambda h, s: back.at[h, s], "gx", gx, 3)

    for h in range(2):
        x1[h][1]()

        def load_column(j, i, h=h):
            return xr1[h, 2 * j + i // 4, pl.ds(i % 4, 4, stride=4), :]

        def store_column(j, i, value, h=h):
            sm[h, pl.ds(8 * j + i, 4, stride=64), :] = value

        vertical(load_column, store_column)
        s_hi, s_lo = split(jnp.concatenate([sm[h, 0:128], sm[h, 128:256]], axis=1))

        def profile(c, carry, h=h, s_hi=s_hi, s_lo=s_lo):
            rows = pl.ds(pl.multiple_of(256 * c, 256), 256)
            value = dot3(w_hi[rows, :], w_lo[rows, :], s_hi, s_lo, ((1,), (1,)))
            p_ref[h, pl.ds(4 * c, 4)] = value.reshape(4, 8, 8, 128)
            return carry

        lax.fori_loop(0, 4, profile, 0)
        o1[h][0]()
        r1[h, gx] = p_ref[h, gx]

    top = lax.broadcasted_iota(jnp.int32, (8, 8, 128), 1) < 4

    def interleave(src, dst, h):
        def pair(p, carry):
            a, b = src[h, 2 * p], src[h, 2 * p + 1]
            dst[h, :, 0, p] = jnp.where(top, a, pltpu.roll(b, 4, 1))
            dst[h, :, 1, p] = jnp.where(top, pltpu.roll(a, 4, 1), b)
            return carry

        lax.fori_loop(0, 8, pair, 0)

    for h in range(2):
        o1[h][1]()
        interleave(r1, t2, h)
        o2[h][0]()
        a_ref[h, gy] = t2[h, gy // 2, gy % 2]
    o2[0][1]()
    o2[1][1]()

    def weigh(c, carry):
        blocks = [a_ref[h, pl.ds(4 * c, 4)].reshape(256, 128) for h in range(2)]
        hi, lo = split(jnp.concatenate(blocks, axis=1))
        value = dot3(hi, lo, e_hi[...], e_lo[...], ((1,), (0,)))
        for h in range(2):
            q_ref[h, pl.ds(4 * c, 4)] = value[:, 128 * h : 128 * h + 128].reshape(4, 8, 8, 128)
        return carry

    lax.fori_loop(0, 4, weigh, 0)
    for h in range(2):
        o3[h][0]()
        b_ref[h, gy] = q_ref[h, gy]
    for h in range(2):
        o3[h][1]()
        interleave(b_ref, u_ref, h)
        o4[h][0]()
        back[h, gx] = u_ref[h, gx // 2, gx % 2]

    for h in range(2):
        o4[h][1]()
        b_hi, b_lo = split(back[h].reshape(1024, 128))
        spread = dot3(b_hi, b_lo, w_hi[...], w_lo[...], ((0,), (0,)))
        sp[h, 0:128] = spread[:, 0:128]
        sp[h, 128:256] = spread[:, 128:256]

        def load_spread(j, i, h=h):
            return sp[h, pl.ds(8 * j + i, 4, stride=64), :]

        def store_spread(j, i, value, h=h):
            xs2[h, 2 * j + i // 4, pl.ds(i % 4, 4, stride=4), :] = value

        vertical(load_spread, store_spread)
        x2[h][0]()
        xr2[h, gx] = xs2[h, gx]

    for h in range(2):
        x2[h][1]()
        for pair in range(2):
            rows = slice(8 * pair, 8 * pair + 8)
            for t in range(8):
                a, b = swap(xr2[h, 2 * t, rows], xr2[h, 2 * t + 1, rows])
                uc[h, 4 + 2 * pair, :, 128 * t : 128 * t + 128] = a
                uc[h, 5 + 2 * pair, :, 128 * t : 128 * t + 128] = b
        second_halo[h][0]()

    sums = (zero_tile(), zero_tile(), zero_tile())
    for h in range(2):
        second_halo[h][1]()
        second_halo[h][2]()
        src = lateral(uc, h)

        def last(i, carry, h=h, src=src):
            pq, rq, qq = carry
            d, r = dir_ref[h, i], res_ref[h, i]
            q = d + stencil(src, h, i + 4)
            image_ref[h, i] = q
            return pq + d * q, rq + r * q, qq + q * q

        sums = lax.fori_loop(0, 4, last, sums)

    def fold(x):
        total = x[:, 0:128]
        for t in range(1, 8):
            total = total + x[:, 128 * t : 128 * t + 128]
        return jnp.sum(total, axis=0, keepdims=True)

    rows = [fold(x) for x in (rr, *sums)]
    part[...] = jnp.concatenate(rows + [jnp.zeros((4, 128), F32)], axis=0)
    g1 = exchange(lambda p: part, lambda s: gat1.at[s], "gx", gx, r_send.at[0], r_recv.at[0])
    g2 = exchange(lambda p: part2, lambda s: gat2.at[s], "gy", gy, r_send.at[1], r_recv.at[1])
    g1[0]()
    gat1[gx] = part[...]
    g1[1]()
    part2[...] = jnp.sum(gat1[...], axis=0)
    g2[0]()
    gat2[gy] = part2[...]
    g2[1]()
    total = jnp.sum(jnp.sum(gat2[...], axis=0), axis=1, keepdims=True)
    norm_now, curvature = total[0:1], total[1:2]
    cross, image_norm = total[2:3], total[3:4]
    alpha = norm_now / curvature
    norm_next = norm_now - 2.0 * alpha * cross + alpha * alpha * image_norm
    beta = norm_next / norm_now
    scal_ref[...] = jnp.concatenate(
        [jnp.broadcast_to(alpha, (4, 128)), jnp.broadcast_to(beta, (4, 128))], axis=0
    )

    coef_halo[2]()
    for h in range(2):
        first_halo[h][2]()
        for group in (x1, x2, o1, o2, o3, o4):
            group[h][2]()
    g1[2]()
    g2[2]()


def per_device(
    direction,
    solution,
    residual,
    north_coef,
    east_coef,
    ocean,
    vert_coef,
    obs_owner,
    obs_row,
    obs_col,
    obs_frac,
    error_inverse,
):
    def by_row(x):
        return x.reshape(2, 2, 4, 4, 1024).transpose(0, 3, 1, 2, 4).reshape(2, 4, 8, 1024)

    coef = jnp.stack([north_coef, east_coef, ocean.astype(F32)])
    owner = obs_owner.reshape(512).astype(F32)
    obs = jnp.stack(
        [
            owner,
            obs_row.reshape(512).astype(F32),
            obs_col.reshape(512).astype(F32),
            obs_frac[0, 0, 0],
            obs_frac[0, 0, 1],
        ],
        axis=1,
    )
    vm = pltpu.VMEM
    dma = pltpu.SemaphoreType.DMA
    obs_buf = vm((2, N, 8, 8, 128), F32)
    mix_buf = vm((2, 8, 2, 8, 8, 128), F32)
    image, scal = pl.pallas_call(
        kernel,
        out_shape=(
            jax.ShapeDtypeStruct((2, 4, 8, 1024), F32),
            jax.ShapeDtypeStruct((8, 128), F32),
        ),
        in_specs=[pl.BlockSpec(memory_space=pltpu.VMEM)] * 7,
        out_specs=(pl.BlockSpec(memory_space=pltpu.VMEM),) * 2,
        scratch_shapes=[
            vm((2, 12, 8, 1024), F32),
            vm((2, 12, 8, 1024), F32),
            vm((2, 12, 8, 1024), F32),
            vm((3, 3, 4, 1024), F32),
            vm((12, 4, 8, 1024), F32),
            vm((64, 4, 128), F32),
            vm((64, 4, 128), F32),
            vm((64, 4, 128), F32),
            vm((64, 4, 128), F32),
            vm((512, 256), BF16),
            vm((512, 256), BF16),
            vm((1024, 256), BF16),
            vm((1024, 256), BF16),
            vm((256, 256), BF16),
            vm((256, 256), BF16),
            vm((2, N, 16, 128), F32),
            vm((2, N, 16, 128), F32),
            vm((2, 256, 128), F32),
            obs_buf,
            obs_buf,
            mix_buf,
            obs_buf,
            obs_buf,
            obs_buf,
            mix_buf,
            obs_buf,
            vm((2, 256, 128), F32),
            vm((2, N, 16, 128), F32),
            vm((2, N, 16, 128), F32),
            vm((8, 128), F32),
            vm((N, 8, 128), F32),
            vm((8, 128), F32),
            vm((N, 8, 128), F32),
            dma((10,)),
            dma((10,)),
            dma((4, N)),
            dma((4, N)),
            dma((8, N)),
            dma((8, N)),
            dma((2, N)),
            dma((2, N)),
        ],
        compiler_params=pltpu.CompilerParams(collective_id=0, has_side_effects=True),
        name="cg_step",
    )(
        by_row(direction),
        by_row(residual),
        coef,
        jnp.repeat(vert_coef.reshape(64, 2, 128), 2, axis=1),
        obs,
        owner.reshape(1, 512),
        error_inverse.reshape(256, 256),
    )
    image = image.reshape(2, 4, 2, 4, 1024).transpose(0, 2, 3, 1, 4).reshape(4, 4, 4, 1024)
    alpha = scal[0, 0]
    beta = scal[4, 0]
    residual_next = residual - alpha * image
    solution_next = solution + alpha * direction
    direction_next = residual_next + beta * direction
    return (solution_next, residual_next, direction_next)


def solution(mesh):
    field = P(None, "gx", "gy", None)
    in_specs = (
        field,
        field,
        field,
        P("gy", None),
        P("gy", None),
        P("gy", None),
        P(None, "gy", "gx"),
        P("gy", "gx", None, None),
        P("gy", "gx", None),
        P("gy", "gx", None),
        P("gy", "gx", None, None),
        P("gy", "gx", None, None),
    )
    return jax.shard_map(
        per_device, mesh=mesh, in_specs=in_specs, out_specs=(field,) * 3, check_vma=False
    )
```

profile of v0, /device:TPU:1, one launch (start us, length us, event | category | flops | bytes accessed | tf_op | source)
XLA Modules:
  0.0 148.3 jit_solution(363053637333867479)
XLA Ops:
  0.6 0.0 copy-start.3
  0.6 1.3 convert_bitcast_fusion.3
  1.9 0.7 convert_bitcast_fusion.1
  2.6 0.8 slice_bitcast_fusion
  3.4 0.7 convert_bitcast_fusion
  4.2 1.4 pad_maximum_fusion.coef_ref
  5.5 0.0 copy-done.3
  5.5 0.1 reshape.85
  5.7 0.0 copy-start.1
  5.7 0.7 broadcast_in_dim.3
  6.3 0.9 copy.28.obs_ref
  7.2 0.0 copy-done.1
  7.2 0.2 copy.32
  7.4 0.0 copy-start
  7.4 0.8 reshape.84.res_ref
  8.2 0.1 copy-done
  8.3 0.2 copy.33
  8.5 0.8 reshape.82.dir_ref
  9.3 132.7 %cg_step.1 = (f32[2,4,8,1024]{3,2,1,0:T(8,128)}, f32[8,128]{1,0:T(8,128)}) custom-call(f32[2,4,8,1024]{3,2,1,0:T(8,128)} %reshape.82.dir_ref, f32[2,4,8,1024]{3,2,1,0:T(8,128)} %reshape.84.res_ref, f32[3,4,1024]{2,1,0:T(4,128)} %pad_maximum_fusion.coef_ref, f32[64,4,128]{2,1,0:T(4,128)} %bitcast.39, f32[512,5]{1,0:T(8,128)} %copy.28.obs_ref, ...), custom_call_target="tpu_custom_call" | custom-call | tf_op jit(solution)/shard_map/cg_step/pallas_call | solution.py:565
  142.0 1.3 fusion
  143.4 1.5 %broadcast_multiply_fusion = f32[2,4,8,1024]{3,2,1,0:T(8,128)S(1)} fusion(f32[2,4,8,1024]{3,2,1,0:T(8,128)} %get-tuple-element.6, f32[]{:T(128)} %bitcast.15), kind=kLoop, calls=%fused_computation.5 | loop fusion | flops 65536 | bytes 524292 | tf_op jit(solution)/shard_map/mul | solution.py:630
  144.9 0.1 mul.31
  145.0 0.0 copy-start.2
  145.0 0.2 copy.29
  145.2 0.8 copy-done.2
  146.0 2.3 %multiply_add_fusion = (f32[4,4,4,1024]{3,2,1,0:T(4,128)}, f32[4,4,4,1024]{3,2,1,0:T(4,128)}, f32[4,4,4,1024]{3,2,1,0:T(4,128)}) fusion(f32[4,4,4,1024]{3,2,1,0:T(4,128)S(1)} %copy-done, f32[]{:T(128)} %bitcast.18, f32[4,4,4,1024]{3,2,1,0:T(4,128)S(1)} %copy-done.1, f32[2,2,4,4,1024]{4,3,2,1,0:T(4,128)S(1)} %copy.29, f32[4,4,4,1024]{3,2,1,0:T(4,128)S(1)} %copy-done.2, ...), kind=kLoop, calls=%fused_computation.3 | loop fusion | flops 327680 | bytes 1835016 | tf_op jit(solution)/shard_map/add | solution.py:632
  (1 shorter events, 0.0 us)
Async XLA Ops:
  0.6 4.9 %copy-start.3 = (f32[64,4,64]{2,1,0:T(4,128)S(1)}, f32[64,4,64]{2,1,0:T(4,128)}, u32[]{:S(2)}) copy-start(f32[64,4,64]{2,1,0:T(4,128)} %param.18) | copy-start | bytes 196612
  5.7 1.6 %copy-start.1 = (f32[4,4,4,1024]{3,2,1,0:T(4,128)S(1)}, f32[4,4,4,1024]{3,2,1,0:T(4,128)}, u32[]{:S(2)}) copy-start(f32[4,4,4,1024]{3,2,1,0:T(4,128)} %param.14) | copy-start | bytes 786436
  7.4 1.0 copy-start
  145.0 1.0 copy-start.2
where the time goes:
time: 149 us; the launch traced here: 148 us
  Pallas kernels  133 us (89%)
  other arithmetic  7.95 us (5%)
  local copies, waits for them, and re-layouts  6.92 us (5%)
    pallas_call x1, Pallas kernels, per_device(): pl.pallas_call(kernel, out_shape=(jax.ShapeDtypeStruct((2, 4, 8, 1024), F...  133 us

commit v1 on v0

--- a/solution.py
+++ b/solution.py
@@ -57,21 +57,33 @@
     return start, wait_recv, wait_send
 
 
+OFFSETS = ((3, -3), (0, 4), (2, -2), (1, -1))
+
+
 def kernel(
     dir_ref,
     res_ref,
-    coef_ref,
+    north_ref,
+    east_ref,
+    ocean_ref,
     vert_ref,
-    obs_ref,
     own_ref,
+    row_ref,
+    col_ref,
+    frac_ref,
     err_ref,
     image_ref,
     scal_ref,
+    dt,
     ua,
     ub,
     uc,
-    hc,
+    hn,
+    he,
+    ho,
     cf,
+    obs_ref,
+    vb,
     inv_ref,
     fa_ref,
     fb_ref,
@@ -104,8 +116,14 @@
     hs_recv,
     x_send,
     x_recv,
-    o_send,
-    o_recv,
+    o1_send,
+    o1_recv,
+    o2_send,
+    o2_recv,
+    o3_send,
+    o3_recv,
+    o4_send,
+    o4_recv,
     r_send,
     r_recv,
 ):
@@ -130,99 +148,27 @@
         return carry
 
     lax.fori_loop(1, N, greet, 0)
-    pl.semaphore_wait(barrier, 2 * (N - 1))
-
-    def halo_copy(src, dst, sem, toward):
-        return pltpu.make_async_remote_copy(
-            src_ref=src,
-            dst_ref=dst,
-            send_sem=hs_send.at[sem],
-            recv_sem=hs_recv.at[sem],
-            device_id={"gy": toward},
-            device_id_type=pl.DeviceIdType.MESH,
-        )
-
-    def halo(src, buf, sem):
-        def up():
-            return halo_copy(src, buf(0), sem, gy + 1)
-
-        def down():
-            return halo_copy(src, buf(2), sem + 1, gy - 1)
-
-        def start():
-            @pl.when(gy < N - 1)
-            def _():
-                up().start()
-
-            @pl.when(gy > 0)
-            def _():
-                down().start()
-
-        def wait_recv():
-            @pl.when(gy > 0)
-            def _():
-                up().wait_recv()
-
-            @pl.when(gy < N - 1)
-            def _():
-                down().wait_recv()
-
-        def wait_send():
-            @pl.when(gy < N - 1)
-            def _():
-                up().wait_send()
-
-            @pl.when(gy > 0)
-            def _():
-                down().wait_send()
-
-        return start, wait_recv, wait_send
-
-    coef_halo = halo(coef_ref, lambda b: hc.at[b], 0)
-    first_halo = [
-        halo(dir_ref.at[h], lambda b, h=h: ua.at[h, pl.ds(4 * b, 4)], 2 + 2 * h)
-        for h in range(2)
-    ]
-    second_halo = [
-        halo(uc.at[h, pl.ds(4, 4)], lambda b, h=h: uc.at[h, pl.ds(4 * b, 4)], 6 + 2 * h)
-        for h in range(2)
-    ]
-    coef_halo[0]()
-    first_halo[0][0]()
-    first_halo[1][0]()
-
-    @pl.when(gy == 0)
-    def _():
-        hc[0] = jnp.zeros((3, 4, 1024), F32)
-        for h in range(2):
-            ua[h, pl.ds(0, 4)] = jnp.zeros((4, 8, 1024), F32)
-            uc[h, pl.ds(0, 4)] = jnp.zeros((4, 8, 1024), F32)
-
-    @pl.when(gy == N - 1)
-    def _():
-        hc[2] = jnp.zeros((3, 4, 1024), F32)
-        for h in range(2):
-            ua[h, pl.ds(8, 4)] = jnp.zeros((4, 8, 1024), F32)
-            uc[h, pl.ds(8, 4)] = jnp.zeros((4, 8, 1024), F32)
-
-    hc[1] = coef_ref[...]
-    ua[:, pl.ds(4, 4)] = dir_ref[...]
-
-    def factor_row(i, carry):
-        v_prev, up_prev = carry
-        v = vert_ref[i]
-        diagonal = 1.0 + v + v_prev + v_prev * up_prev
-        inverse = 1.0 / diagonal
-        ratio = v * inverse
-        inv_ref[i] = inverse
-        fa_ref[i] = v_prev * inverse
-        fb_ref[i] = ratio
-        return v, -ratio
-
-    zero_row = jnp.zeros((4, 128), F32)
-    lax.fori_loop(0, 64, factor_row, (zero_row, zero_row))
-
-    owner_row = own_ref[0:1, :]
+
+    for h in range(2):
+        for r in range(4):
+            rows = [dir_ref[2 * h + v, l, r : r + 1, :] for v in range(2) for l in range(4)]
+            tile = jnp.concatenate(rows, axis=0)
+            dt[h, r] = tile
+            ua[h, 4 + r] = tile
+
+    owner_row = own_ref[...].astype(F32)
+    table = jnp.concatenate(
+        [
+            owner_row,
+            row_ref[...].astype(F32),
+            col_ref[...].astype(F32),
+            frac_ref[...],
+            jnp.zeros((123, 512), F32),
+        ],
+        axis=0,
+    )
+    for g in range(4):
+        obs_ref[128 * g : 128 * g + 128, :] = table[:, 128 * g : 128 * g + 128].T
     lane512 = lax.broadcasted_iota(jnp.int32, (64, 512), 1)
     sub512 = lax.broadcasted_iota(jnp.int32, (64, 512), 0)
     cell = lax.broadcasted_iota(jnp.int32, (64, 256), 1)
@@ -243,7 +189,7 @@
         return rank + jnp.sum(jnp.where(same, 1.0, 0.0), axis=0, keepdims=True)
 
     rank = lax.fori_loop(0, 8, obs_group, jnp.zeros((1, 512), F32))
-    owner_int = owner_row.astype(jnp.int32)
+    owner_int = own_ref[...]
     slot = ((owner_int % N) * N + owner_int // N) * 4 + rank.astype(jnp.int32)
 
     def slot_group(g, carry):
@@ -260,19 +206,131 @@
     e_hi[...] = hi
     e_lo[...] = lo
 
+    pl.semaphore_wait(barrier, 2 * (N - 1))
+
+    def halo_copy(src, dst, sem, toward):
+        return pltpu.make_async_remote_copy(
+            src_ref=src,
+            dst_ref=dst,
+            send_sem=hs_send.at[sem],
+            recv_sem=hs_recv.at[sem],
+            device_id={"gy": toward},
+            device_id_type=pl.DeviceIdType.MESH,
+        )
+
+    def halo(src, buf, sem):
+        def up():
+            return halo_copy(src, buf(0), sem, gy + 1)
+
+        def down():
+            return halo_copy(src, buf(2), sem + 1, gy - 1)
+
+        def start():
+            @pl.when(gy < N - 1)
+            def _():
+                up().start()
+
+            @pl.when(gy > 0)
+            def _():
+                down().start()
+
+        def wait_recv():
+            @pl.when(gy > 0)
+            def _():
+                up().wait_recv()
+
+            @pl.when(gy < N - 1)
+            def _():
+                down().wait_recv()
+
+        def wait_send():
+            @pl.when(gy < N - 1)
+            def _():
+                up().wait_send()
+
+            @pl.when(gy > 0)
+            def _():
+                down().wait_send()
+
+        return start, wait_recv, wait_send
+
+    coef_halos = [
+        halo(north_ref, lambda b: hn.at[b], 0),
+        halo(east_ref, lambda b: he.at[b], 2),
+        halo(ocean_ref, lambda b: ho.at[b], 4),
+    ]
+    first_halo = [
+        halo(dt.at[h], lambda b, h=h: ua.at[h, pl.ds(4 * b, 4)], 6 + 2 * h) for h in range(2)
+    ]
+    second_halo = [
+        halo(uc.at[h, pl.ds(4, 4)], lambda b, h=h: uc.at[h, pl.ds(4 * b, 4)], 10 + 2 * h)
+        for h in range(2)
+    ]
+    for group in coef_halos:
+        group[0]()
+    first_halo[0][0]()
+    first_halo[1][0]()
+
+    @pl.when(gy == 0)
+    def _():
+        hn[0] = jnp.zeros((4, 1024), F32)
+        he[0] = jnp.zeros((4, 1024), F32)
+        ho[0] = jnp.zeros((4, 1024), jnp.int32)
+        for h in range(2):
+            ua[h, pl.ds(0, 4)] = jnp.zeros((4, 8, 1024), F32)
+            uc[h, pl.ds(0, 4)] = jnp.zeros((4, 8, 1024), F32)
+
+    @pl.when(gy == N - 1)
+    def _():
+        hn[2] = jnp.zeros((4, 1024), F32)
+        he[2] = jnp.zeros((4, 1024), F32)
+        ho[2] = jnp.zeros((4, 1024), jnp.int32)
+        for h in range(2):
+            ua[h, pl.ds(8, 4)] = jnp.zeros((4, 8, 1024), F32)
+            uc[h, pl.ds(8, 4)] = jnp.zeros((4, 8, 1024), F32)
+
+    hn[1] = north_ref[...]
+    he[1] = east_ref[...]
+    ho[1] = ocean_ref[...]
+
+    def spread_row(i, carry):
+        v = vert_ref[i]
+        left = jnp.concatenate([v[0:1], v[0:1], v[2:3], v[2:3]], axis=0)
+        right = jnp.concatenate([v[1:2], v[1:2], v[3:4], v[3:4]], axis=0)
+        vb[i] = jnp.concatenate([left, right], axis=1)
+        return carry
+
+    lax.fori_loop(0, 64, spread_row, 0)
+
+    def factor_row(i, carry):
+        v_prev, up_prev = carry
+        v = vb[i]
+        diagonal = 1.0 + v + v_prev + v_prev * up_prev
+        inverse = 1.0 / diagonal
+        ratio = v * inverse
+        inv_ref[i] = inverse
+        fa_ref[i] = v_prev * inverse
+        fb_ref[i] = ratio
+        return v, -ratio
+
+    zero_row = jnp.zeros((4, 128), F32)
+    lax.fori_loop(0, 64, factor_row, (zero_row, zero_row))
+
     def zero_tile():
-        return jnp.zeros((8, 1024), F32)
+        return jnp.zeros((4, 1024), F32)
 
     def rr_group(i, acc):
         x = res_ref[i // 4, i % 4]
         return acc + x * x
 
-    rr = lax.fori_loop(0, 8, rr_group, zero_tile())
-
-    coef_halo[1]()
+    rr = lax.fori_loop(0, 16, rr_group, zero_tile())
+
+    for group in coef_halos:
+        group[1]()
 
     def coef_row(i, q):
-        return hc[i // 4, q, i % 4 : i % 4 + 1, :]
+        buf = (hn, he, ho)[q]
+        return buf[i // 4, i % 4 : i % 4 + 1, :].astype(F32)
 
     fn_prev = jnp.zeros((1, 1024), F32)
     for i in range(12):
@@ -374,23 +432,65 @@
 
         lax.fori_loop(0, 8, backward, zero_row)
 
-    def obs_exchange(src, dst, axis, me, k):
-        return [
+    z = gx // 2
+    core = gx % 2
+
+    def chip(off):
+        return lax.rem(z + off + 8, 8)
+
+    def o1_copy(h, peer, slot):
+        return pltpu.make_async_remote_copy(
+            src_ref=p_ref.at[h, peer],
+            dst_ref=r1.at[h, slot],
+            send_sem=o1_send.at[h, peer],
+            recv_sem=o1_recv.at[h, slot],
+            device_id={"gx": peer},
+            device_id_type=pl.DeviceIdType.MESH,
+        )
+
+    def o4_copy(h, c, s, k, peer, slot):
+        return pltpu.make_async_remote_copy(
+            src_ref=u_ref.at[c, s, k, h],
+            dst_ref=back.at[h, slot],
+            send_sem=o4_send.at[h, peer],
+            recv_sem=o4_recv.at[h, slot],
+            device_id={"gx": peer},
+            device_id_type=pl.DeviceIdType.MESH,
+        )
+
+    def peers(c, s, step):
+        off = OFFSETS[c][s]
+        if off == 0:
+            step(1 - core, 2 * z + 1 - core)
+        else:
+            for k in range(2):
+                step(k, 2 * chip(off) + k)
+
+    o2 = [
+        [
             exchange(
-                lambda p, h=h: src(h, p),
-                lambda s, h=h: dst(h, s),
-                axis,
-                me,
-                o_send.at[2 * k + h],
-                o_recv.at[2 * k + h],
+                lambda p, h=h, c=c: t2.at[h, p // 2, p % 2, c],
+                lambda s, h=h, c=c: a_ref.at[h, c, s],
+                "gy",
+                gy,
+                o2_send.at[h, c],
+                o2_recv.at[h, c],
             )
-            for h in range(2)
+            for c in range(4)
         ]
-
-    o1 = obs_exchange(lambda h, p: p_ref.at[h, p], lambda h, s: r1.at[h, s], "gx", gx, 0)
-    o2 = obs_exchange(lambda h, p: t2.at[h, p // 2, p % 2], lambda h, s: a_ref.at[h, s], "gy", gy, 1)
-    o3 = obs_exchange(lambda h, p: q_ref.at[h, p], lambda h, s: b_ref.at[h, s], "gy", gy, 2)
-    o4 = obs_exchange(lambda h, p: u_ref.at[h, p // 2, p % 2], lambda h, s: back.at[h, s], "gx", gx, 3)
+        for h in range(2)
+    ]
+    o3 = [
+        exchange(
+            lambda p, c=c: q_ref.at[c, p],
+            lambda s, c=c: b_ref.at[c, s // 2, s % 2],
+            "gy",
+            gy,
+            o3_send.at[c],
+            o3_recv.at[c],
+        )
+        for c in range(4)
+    ]
 
     for h in range(2):
         x1[h][1]()
@@ -404,55 +504,80 @@
         vertical(load_column, store_column)
         s_hi, s_lo = split(jnp.concatenate([sm[h, 0:128], sm[h, 128:256]], axis=1))
 
-        def profile(c, carry, h=h, s_hi=s_hi, s_lo=s_lo):
-            rows = pl.ds(pl.multiple_of(256 * c, 256), 256)
-            value = dot3(w_hi[rows, :], w_lo[rows, :], s_hi, s_lo, ((1,), (1,)))
-            p_ref[h, pl.ds(4 * c, 4)] = value.reshape(4, 8, 8, 128)
-            return carry
-
-        lax.fori_loop(0, 4, profile, 0)
-        o1[h][0]()
+        for c in range(4):
+            for s in range(2):
+                j = chip(OFFSETS[c][s])
+                rows = pl.ds(pl.multiple_of(128 * j, 128), 128)
+                value = dot3(w_hi[rows, :], w_lo[rows, :], s_hi, s_lo, ((1,), (1,)))
+                p_ref[h, pl.ds(2 * j, 2)] = value.reshape(2, 8, 8, 128)
+                peers(c, s, lambda k, peer: o1_copy(h, peer, gx).start())
         r1[h, gx] = p_ref[h, gx]
 
     top = lax.broadcasted_iota(jnp.int32, (8, 8, 128), 1) < 4
 
-    def interleave(src, dst, h):
-        def pair(p, carry):
-            a, b = src[h, 2 * p], src[h, 2 * p + 1]
-            dst[h, :, 0, p] = jnp.where(top, a, pltpu.roll(b, 4, 1))
-            dst[h, :, 1, p] = jnp.where(top, pltpu.roll(a, 4, 1), b)
-            return carry
-
-        lax.fori_loop(0, 8, pair, 0)
-
-    for h in range(2):
-        o1[h][1]()
-        interleave(r1, t2, h)
-        o2[h][0]()
-        a_ref[h, gy] = t2[h, gy // 2, gy % 2]
-    o2[0][1]()
-    o2[1][1]()
-
-    def weigh(c, carry):
-        blocks = [a_ref[h, pl.ds(4 * c, 4)].reshape(256, 128) for h in range(2)]
+    def mix(a, b):
+        return (
+            jnp.where(top, a, pltpu.roll(b, 4, 1)),
+            jnp.where(top, pltpu.roll(a, 4, 1), b),
+        )
+
+    def forward_chunk(h, c):
+        for s in range(2):
+            peers(c, s, lambda k, peer: o1_copy(h, peer, peer).wait_recv())
+            j = chip(OFFSETS[c][s])
+            even, odd = mix(r1[h, 2 * j], r1[h, 2 * j + 1])
+            t2[h, :, 0, c, s] = even
+            t2[h, :, 1, c, s] = odd
+        o2[h][c][0]()
+        a_ref[h, c, gy] = t2[h, gy // 2, gy % 2, c]
+
+    def weigh(c):
+        o2[0][c][1]()
+        o2[1][c][1]()
+        blocks = [a_ref[h, c].reshape(256, 128) for h in range(2)]
         hi, lo = split(jnp.concatenate(blocks, axis=1))
         value = dot3(hi, lo, e_hi[...], e_lo[...], ((1,), (0,)))
         for h in range(2):
-            q_ref[h, pl.ds(4 * c, 4)] = value[:, 128 * h : 128 * h + 128].reshape(4, 8, 8, 128)
-        return carry
-
-    lax.fori_loop(0, 4, weigh, 0)
+            q_ref[c, :, h] = value[:, 128 * h : 128 * h + 128].reshape(N, 2, 8, 128)
+        o3[c][0]()
+        b_ref[c, gy // 2, gy % 2] = q_ref[c, gy]
+
+    def return_chunk(c):
+        o3[c][1]()
+        for h in range(2):
+            for s in range(2):
+                even, odd = mix(b_ref[c, :, 0, h, s], b_ref[c, :, 1, h, s])
+                u_ref[c, s, 0, h] = even
+                u_ref[c, s, 1, h] = odd
+        send_back(c, 0)
+
+    def send_back(c, h):
+        for s in range(2):
+            peers(c, s, lambda k, peer: o4_copy(h, c, s, k, peer, gx).start())
+            if OFFSETS[c][s] == 0:
+                back[h, gx] = u_ref[c, s, core, h]
+
+    for c in range(4):
+        forward_chunk(0, c)
+    forward_chunk(1, 0)
+    forward_chunk(1, 1)
+    weigh(0)
+    forward_chunk(1, 2)
+    weigh(1)
+    return_chunk(0)
+    forward_chunk(1, 3)
+    weigh(2)
+    return_chunk(1)
+    weigh(3)
+    return_chunk(2)
+    return_chunk(3)
+    for c in range(4):
+        send_back(c, 1)
+
     for h in range(2):
-        o3[h][0]()
-        b_ref[h, gy] = q_ref[h, gy]
-    for h in range(2):
-        o3[h][1]()
-        interleave(b_ref, u_ref, h)
-        o4[h][0]()
-        back[h, gx] = u_ref[h, gx // 2, gx % 2]
-
-    for h in range(2):
-        o4[h][1]()
+        for c in range(4):
+            for s in range(2):
+                peers(c, s, lambda k, peer: o4_copy(h, c, s, k, peer, peer).wait_recv())
         b_hi, b_lo = split(back[h].reshape(1024, 128))
         spread = dot3(b_hi, b_lo, w_hi[...], w_lo[...], ((0,), (0,)))
         sp[h, 0:128] = spread[:, 0:128]
@@ -478,20 +603,26 @@
                 uc[h, 5 + 2 * pair, :, 128 * t : 128 * t + 128] = b
         second_halo[h][0]()
 
-    sums = (zero_tile(), zero_tile(), zero_tile())
     for h in range(2):
         second_halo[h][1]()
         second_halo[h][2]()
         src = lateral(uc, h)
-
-        def last(i, carry, h=h, src=src):
-            pq, rq, qq = carry
-            d, r = dir_ref[h, i], res_ref[h, i]
-            q = d + stencil(src, h, i + 4)
-            image_ref[h, i] = q
-            return pq + d * q, rq + r * q, qq + q * q
-
-        sums = lax.fori_loop(0, 4, last, sums)
+        for r in range(4):
+            tile = stencil(src, h, 4 + r)
+            for v in range(2):
+                for l in range(4):
+                    k = 4 * v + l
+                    image_ref[2 * h + v, l, r : r + 1, :] = tile[k : k + 1]
+
+    def last(i, carry):
+        pq, rq, qq = carry
+        v, l = i // 4, i % 4
+        d, r = dir_ref[v, l], res_ref[v, l]
+        q = d + image_ref[v, l]
+        image_ref[v, l] = q
+        return pq + d * q, rq + r * q, qq + q * q
+
+    sums = lax.fori_loop(0, 16, last, (zero_tile(), zero_tile(), zero_tile()))
 
     def fold(x):
         total = x[:, 0:128]
@@ -520,13 +651,37 @@
         [jnp.broadcast_to(alpha, (4, 128)), jnp.broadcast_to(beta, (4, 128))], axis=0
     )
 
-    coef_halo[2]()
+    for group in coef_halos:
+        group[2]()
     for h in range(2):
         first_halo[h][2]()
-        for group in (x1, x2, o1, o2, o3, o4):
-            group[h][2]()
+        x1[h][2]()
+        x2[h][2]()
+        for c in range(4):
+            o2[h][c][2]()
+            for s in range(2):
+                peers(c, s, lambda k, peer: o1_copy(h, peer, gx).wait_send())
+                peers(c, s, lambda k, peer: o4_copy(h, c, s, k, peer, gx).wait_send())
+    for c in range(4):
+        o3[c][2]()
     g1[2]()
     g2[2]()
+
+
+def update(image_ref, scal_ref, dir_ref, sol_ref, res_ref, sol_out, res_out, dir_out):
+    alpha = scal_ref[0:1, 0:1]
+    beta = scal_ref[4:5, 0:1]
+
+    def each(i, carry):
+        v, l = i // 4, i % 4
+        d = dir_ref[v, l]
+        r = res_ref[v, l] - alpha * image_ref[v, l]
+        sol_out[v, l] = sol_ref[v, l] + alpha * d
+        res_out[v, l] = r
+        dir_out[v, l] = r + beta * d
+        return carry
+
+    lax.fori_loop(0, 16, each, 0)
 
 
 def per_device(
@@ -543,94 +698,94 @@
     obs_frac,
     error_inverse,
 ):
-    def by_row(x):
-        return x.reshape(2, 2, 4, 4, 1024).transpose(0, 3, 1, 2, 4).reshape(2, 4, 8, 1024)
-
-    coef = jnp.stack([north_coef, east_coef, ocean.astype(F32)])
-    owner = obs_owner.reshape(512).astype(F32)
-    obs = jnp.stack(
-        [
-            owner,
-            obs_row.reshape(512).astype(F32),
-            obs_col.reshape(512).astype(F32),
-            obs_frac[0, 0, 0],
-            obs_frac[0, 0, 1],
-        ],
-        axis=1,
-    )
     vm = pltpu.VMEM
     dma = pltpu.SemaphoreType.DMA
-    obs_buf = vm((2, N, 8, 8, 128), F32)
-    mix_buf = vm((2, 8, 2, 8, 8, 128), F32)
+    field = jax.ShapeDtypeStruct((4, 4, 4, 1024), F32)
+    in_vmem = pl.BlockSpec(memory_space=pltpu.VMEM)
+    level = vm((64, 4, 128), F32)
+    wide = vm((2, 12, 8, 1024), F32)
+    swap_buf = vm((2, N, 16, 128), F32)
     image, scal = pl.pallas_call(
         kernel,
-        out_shape=(
-            jax.ShapeDtypeStruct((2, 4, 8, 1024), F32),
-            jax.ShapeDtypeStruct((8, 128), F32),
-        ),
-        in_specs=[pl.BlockSpec(memory_space=pltpu.VMEM)] * 7,
-        out_specs=(pl.BlockSpec(memory_space=pltpu.VMEM),) * 2,
+        out_shape=(field, jax.ShapeDtypeStruct((8, 128), F32)),
+        in_specs=[in_vmem] * 11,
+        out_specs=(in_vmem,) * 2,
         scratch_shapes=[
-            vm((2, 12, 8, 1024), F32),
-            vm((2, 12, 8, 1024), F32),
-            vm((2, 12, 8, 1024), F32),
-            vm((3, 3, 4, 1024), F32),
+            vm((2, 4, 8, 1024), F32),
+            wide,
+            wide,
+            wide,
+            vm((3, 4, 1024), F32),
+            vm((3, 4, 1024), F32),
+            vm((3, 4, 1024), jnp.int32),
             vm((12, 4, 8, 1024), F32),
-            vm((64, 4, 128), F32),
-            vm((64, 4, 128), F32),
-            vm((64, 4, 128), F32),
-            vm((64, 4, 128), F32),
+            vm((512, 128), F32),
+            level,
+            level,
+            level,
+            level,
+            level,
             vm((512, 256), BF16),
             vm((512, 256), BF16),
             vm((1024, 256), BF16),
             vm((1024, 256), BF16),
             vm((256, 256), BF16),
             vm((256, 256), BF16),
-            vm((2, N, 16, 128), F32),
-            vm((2, N, 16, 128), F32),
+            swap_buf,
+            swap_buf,
             vm((2, 256, 128), F32),
-            obs_buf,
-            obs_buf,
-            mix_buf,
-            obs_buf,
-            obs_buf,
-            obs_buf,
-            mix_buf,
-            obs_buf,
+            vm((2, N, 8, 8, 128), F32),
+            vm((2, N, 8, 8, 128), F32),
+            vm((2, 8, 2, 4, 2, 8, 128), F32),
+            vm((2, 4, N, 2, 8, 128), F32),
+            vm((4, N, 2, 2, 8, 128), F32),
+            vm((4, 8, 2, 2, 2, 8, 128), F32),
+            vm((4, 2, 2, 2, 8, 8, 128), F32),
+            vm((2, N, 8, 8, 128), F32),
             vm((2, 256, 128), F32),
-            vm((2, N, 16, 128), F32),
-            vm((2, N, 16, 128), F32),
+            swap_buf,
+            swap_buf,
             vm((8, 128), F32),
             vm((N, 8, 128), F32),
             vm((8, 128), F32),
             vm((N, 8, 128), F32),
-            dma((10,)),
-            dma((10,)),
+            dma((14,)),
+            dma((14,)),
             dma((4, N)),
             dma((4, N)),
-            dma((8, N)),
-            dma((8, N)),
+            dma((2, N)),
+            dma((2, N)),
+            dma((2, 4, N)),
+            dma((2, 4, N)),
+            dma((4, N)),
+            dma((4, N)),
+            dma((2, N)),
+            dma((2, N)),
             dma((2, N)),
             dma((2, N)),
         ],
         compiler_params=pltpu.CompilerParams(collective_id=0, has_side_effects=True),
         name="cg_step",
     )(
-        by_row(direction),
-        by_row(residual),
-        coef,
-        jnp.repeat(vert_coef.reshape(64, 2, 128), 2, axis=1),
-        obs,
-        owner.reshape(1, 512),
+        direction,
+        residual,
+        north_coef,
+        east_coef,
+        ocean,
+        vert_coef,
+        obs_owner.reshape(1, 512),
+        obs_row.reshape(1, 512),
+        obs_col.reshape(1, 512),
+        obs_frac.reshape(2, 512),
         error_inverse.reshape(256, 256),
     )
-    image = image.reshape(2, 4, 2, 4, 1024).transpose(0, 2, 3, 1, 4).reshape(4, 4, 4, 1024)
-    alpha = scal[0, 0]
-    beta = scal[4, 0]
-    residual_next = residual - alpha * image
-    solution_next = solution + alpha * direction
-    direction_next = residual_next + beta * direction
-    return (solution_next, residual_next, direction_next)
+    return pl.pallas_call(
+        update,
+        out_shape=(field,) * 3,
+        in_specs=[in_vmem] * 5,
+        out_specs=(in_vmem,) * 3,
+        name="cg_update",
+    )(image, scal, direction, solution, residual)
 
 
 def solution(mesh):

time: 149 us -> 127 us (0.85)
  other arithmetic: 7.95 us -> 0 us
  Pallas kernels: 133 us -> 126 us
  local copies, waits for them, and re-layouts: 6.92 us -> 0 us
    pallas_call x1 -> x2, Pallas kernels: 133 us -> 126 us  [the longest x1 123 us: per_device(): pl.pallas_call(kernel, out_shape=(field, jax.ShapeDtypeStruct((8, 128), F...]
    add x1 -> x0, other arithmetic: 2.33 us -> none  [per_device(): direction_next = residual_next + beta * direction]
    another operation x2 -> x0, other arithmetic: 2.09 us -> none  [per_device(): coef = jnp.stack([north_coef, east_coef, ocean.astype(F32)])]
    reshape x5 -> x0, local copies, waits for them, and re-layouts: 2.05 us -> none  [the longest x4 1.93 us: by_row(): x.reshape(2, 2, 4, 4, 1024).transpose(0, 3, 1, 2, 4).reshape(2, 4, 8, 1024)]
    convert_element_type x2 -> x0, other arithmetic: 2 us -> none  [the longest x1 1.3 us: per_device(): owner = obs_owner.reshape(512).astype(F32)]
    another operation x3 -> x0, local copies, waits for them, and re-layouts: 1.65 us -> none  [per_device(): jnp.stack([owner, obs_row.reshape(512).astype(F32), obs_col.reshape(512)....]
    mul x1 -> x0, other arithmetic: 1.54 us -> none  [per_device(): residual_next = residual - alpha * image]
where the time goes in v1:
time: 127 us
  Pallas kernels  126 us (99%)
    pallas_call x1, Pallas kernels, per_device(): pl.pallas_call(kernel, out_shape=(field, jax.ShapeDtypeStruct((8, 128), F...  123 us
    pallas_call x1, Pallas kernels, per_device(): pl.pallas_call(update, out_shape=(field,) * 3, in_specs=[in_vmem] * 5, ou...  2.7 us

profile of v1, /device:TPU:1, one launch (start us, length us, event | category | flops | bytes accessed | tf_op | source)
XLA Modules:
  0.0 126.6 jit_solution(6639644197003009554)
XLA Ops:
  0.6 123.2 %cg_step.1 = (f32[4,4,4,1024]{3,2,1,0:T(4,128)}, f32[8,128]{1,0:T(8,128)}) custom-call(f32[4,4,4,1024]{3,2,1,0:T(4,128)} %dir_ref.3, f32[4,4,4,1024]{3,2,1,0:T(4,128)} %res_ref.3, f32[4,1024]{1,0:T(4,128)} %north_ref.1, f32[4,1024]{1,0:T(4,128)} %east_ref.1, s32[4,1024]{1,0:T(4,128)} %ocean_ref.1, f32[64,4,64]{2,1,0:T(4,128)} %vert_ref.1, s32[1,512]{1,0:T(1,128)} %bitcast.7, ...), custom_call_target="tpu_custom_call" | custom-call | tf_op jit(solution)/shard_map/cg_step/pallas_call | solution.py:708
  123.9 2.7 %cg_update.1 = (f32[4,4,4,1024]{3,2,1,0:T(4,128)}, f32[4,4,4,1024]{3,2,1,0:T(4,128)}, f32[4,4,4,1024]{3,2,1,0:T(4,128)}) custom-call(f32[4,4,4,1024]{3,2,1,0:T(4,128)} %get-tuple-element.5.image_ref, f32[8,128]{1,0:T(8,128)} %get-tuple-element.6.scal_ref, f32[4,4,4,1024]{3,2,1,0:T(4,128)} %dir_ref.3, f32[4,4,4,1024]{3,2,1,0:T(4,128)} %sol_ref.1, ...), custom_call_target="tpu_custom_call" | custom-call | tf_op jit(solution)/shard_map/cg_update/pallas_call | solution.py:782

commit v2 on v1

--- a/solution.py
+++ b/solution.py
@@ -57,7 +57,7 @@
     return start, wait_recv, wait_send
 
 
-OFFSETS = ((3, -3), (0, 4), (2, -2), (1, -1))
+OFFSETS = ((1, -1), (2, -2), (0, 4), (3, -3))
 
 
 def kernel(
@@ -92,6 +92,8 @@
     c_lo,
     w_hi,
     w_lo,
+    wt_hi,
+    wt_lo,
     e_hi,
     e_lo,
     xs1,
@@ -197,8 +199,10 @@
         sub = lax.broadcasted_iota(jnp.int32, (256, 512), 0) + base
         hot = jnp.where(sub == slot, 1.0, 0.0).astype(BF16)
         rows = pl.ds(base, 256)
-        w_hi[rows, :] = dot(hot, c_hi[...], ((1,), (0,))).astype(BF16)
-        w_lo[rows, :] = dot(hot, c_lo[...], ((1,), (0,))).astype(BF16)
+        for src, dst, dst_t in ((c_hi, w_hi, wt_hi), (c_lo, w_lo, wt_lo)):
+            value = dot(hot, src[...], ((1,), (0,)))
+            dst[rows, :] = value.astype(BF16)
+            dst_t[:, rows] = value.T.astype(BF16)
         return carry
 
     lax.fori_loop(0, 4, slot_group, 0)
@@ -293,14 +297,15 @@
     he[1] = east_ref[...]
     ho[1] = ocean_ref[...]
 
-    def spread_row(i, carry):
-        v = vert_ref[i]
-        left = jnp.concatenate([v[0:1], v[0:1], v[2:3], v[2:3]], axis=0)
-        right = jnp.concatenate([v[1:2], v[1:2], v[3:4], v[3:4]], axis=0)
-        vb[i] = jnp.concatenate([left, right], axis=1)
+    def spread_rows(j, carry):
+        for i in range(8):
+            v = vert_ref[8 * j + i]
+            left = jnp.concatenate([v[0:1], v[0:1], v[2:3], v[2:3]], axis=0)
+            right = jnp.concatenate([v[1:2], v[1:2], v[3:4], v[3:4]], axis=0)
+            vb[8 * j + i] = jnp.concatenate([left, right], axis=1)
         return carry
 
-    lax.fori_loop(0, 64, spread_row, 0)
+    lax.fori_loop(0, 8, spread_rows, 0)
 
     def factor_row(i, carry):
         v_prev, up_prev = carry
@@ -360,11 +365,8 @@
         src, dst = buf, ub
         for step in range(NSTEP - 1):
 
-            def row(i, carry, src=src, dst=dst):
+            for i in range(1 + step, 11 - step):
                 dst[h, i] = stencil(src, h, i)
-                return carry
-
-            lax.fori_loop(1 + step, 11 - step, row, 0)
             src, dst = dst, src
         return src
 
@@ -467,18 +469,15 @@
                 step(k, 2 * chip(off) + k)
 
     o2 = [
-        [
-            exchange(
-                lambda p, h=h, c=c: t2.at[h, p // 2, p % 2, c],
-                lambda s, h=h, c=c: a_ref.at[h, c, s],
-                "gy",
-                gy,
-                o2_send.at[h, c],
-                o2_recv.at[h, c],
-            )
-            for c in range(4)
-        ]
-        for h in range(2)
+        exchange(
+            lambda p, c=c: t2.at[p // 2, p % 2, c],
+            lambda s, c=c: a_ref.at[c, s],
+            "gy",
+            gy,
+            o2_send.at[c],
+            o2_recv.at[c],
+        )
+        for c in range(4)
     ]
     o3 = [
         exchange(
@@ -492,25 +491,34 @@
         for c in range(4)
     ]
 
+    def columns(h):
+        x1[h][1]()
+
+        def load_column(j, i):
+            return xr1[h, 2 * j + i // 4, pl.ds(i % 4, 4, stride=4), :]
+
+        def store_column(j, i, value):
+            sm[h, pl.ds(8 * j + i, 4, stride=64), :] = value
+
+        vertical(load_column, store_column)
+        return split(jnp.concatenate([sm[h, 0:128], sm[h, 128:256]], axis=1))
+
+    def profile(h, c, smoothed):
+        for s in range(2):
+            j = chip(OFFSETS[c][s])
+            rows = pl.ds(pl.multiple_of(128 * j, 128), 128)
+            value = dot3(w_hi[rows, :], w_lo[rows, :], *smoothed, ((1,), (1,)))
+            p_ref[h, pl.ds(2 * j, 2)] = value.reshape(2, 8, 8, 128)
+            peers(c, s, lambda k, peer: o1_copy(h, peer, gx).start())
+
+    smoothed_0 = columns(0)
+    profile(0, 0, smoothed_0)
+    smoothed_1 = columns(1)
+    profile(1, 0, smoothed_1)
+    for c in range(1, 4):
+        profile(0, c, smoothed_0)
+        profile(1, c, smoothed_1)
     for h in range(2):
-        x1[h][1]()
-
-        def load_column(j, i, h=h):
-            return xr1[h, 2 * j + i // 4, pl.ds(i % 4, 4, stride=4), :]
-
-        def store_column(j, i, value, h=h):
-            sm[h, pl.ds(8 * j + i, 4, stride=64), :] = value
-
-        vertical(load_column, store_column)
-        s_hi, s_lo = split(jnp.concatenate([sm[h, 0:128], sm[h, 128:256]], axis=1))
-
-        for c in range(4):
-            for s in range(2):
-                j = chip(OFFSETS[c][s])
-                rows = pl.ds(pl.multiple_of(128 * j, 128), 128)
-                value = dot3(w_hi[rows, :], w_lo[rows, :], s_hi, s_lo, ((1,), (1,)))
-                p_ref[h, pl.ds(2 * j, 2)] = value.reshape(2, 8, 8, 128)
-                peers(c, s, lambda k, peer: o1_copy(h, peer, gx).start())
         r1[h, gx] = p_ref[h, gx]
 
     top = lax.broadcasted_iota(jnp.int32, (8, 8, 128), 1) < 4
@@ -521,20 +529,20 @@
             jnp.where(top, pltpu.roll(a, 4, 1), b),
         )
 
-    def forward_chunk(h, c):
-        for s in range(2):
-            peers(c, s, lambda k, peer: o1_copy(h, peer, peer).wait_recv())
-            j = chip(OFFSETS[c][s])
-            even, odd = mix(r1[h, 2 * j], r1[h, 2 * j + 1])
-            t2[h, :, 0, c, s] = even
-            t2[h, :, 1, c, s] = odd
-        o2[h][c][0]()
-        a_ref[h, c, gy] = t2[h, gy // 2, gy % 2, c]
+    def forward_chunk(c):
+        for h in range(2):
+            for s in range(2):
+                peers(c, s, lambda k, peer: o1_copy(h, peer, peer).wait_recv())
+                j = chip(OFFSETS[c][s])
+                even, odd = mix(r1[h, 2 * j], r1[h, 2 * j + 1])
+                t2[:, 0, c, h, s] = even
+                t2[:, 1, c, h, s] = odd
+        o2[c][0]()
+        a_ref[c, gy] = t2[gy // 2, gy % 2, c]
 
     def weigh(c):
-        o2[0][c][1]()
-        o2[1][c][1]()
-        blocks = [a_ref[h, c].reshape(256, 128) for h in range(2)]
+        o2[c][1]()
+        blocks = [a_ref[c, :, h].reshape(256, 128) for h in range(2)]
         hi, lo = split(jnp.concatenate(blocks, axis=1))
         value = dot3(hi, lo, e_hi[...], e_lo[...], ((1,), (0,)))
         for h in range(2):
@@ -549,7 +557,6 @@
                 even, odd = mix(b_ref[c, :, 0, h, s], b_ref[c, :, 1, h, s])
                 u_ref[c, s, 0, h] = even
                 u_ref[c, s, 1, h] = odd
-        send_back(c, 0)
 
     def send_back(c, h):
         for s in range(2):
@@ -557,31 +564,35 @@
             if OFFSETS[c][s] == 0:
                 back[h, gx] = u_ref[c, s, core, h]
 
-    for c in range(4):
-        forward_chunk(0, c)
-    forward_chunk(1, 0)
-    forward_chunk(1, 1)
+    def back_chunk(c):
+        return_chunk(c)
+        for h in range(2):
+            send_back(c, h)
+
+    forward_chunk(0)
+    forward_chunk(1)
     weigh(0)
-    forward_chunk(1, 2)
+    forward_chunk(2)
     weigh(1)
-    return_chunk(0)
-    forward_chunk(1, 3)
+    back_chunk(0)
+    forward_chunk(3)
     weigh(2)
-    return_chunk(1)
+    back_chunk(1)
     weigh(3)
-    return_chunk(2)
-    return_chunk(3)
-    for c in range(4):
-        send_back(c, 1)
+    back_chunk(2)
+    back_chunk(3)
 
     for h in range(2):
+        spread = jnp.zeros((256, 128), F32)
         for c in range(4):
             for s in range(2):
                 peers(c, s, lambda k, peer: o4_copy(h, c, s, k, peer, peer).wait_recv())
-        b_hi, b_lo = split(back[h].reshape(1024, 128))
-        spread = dot3(b_hi, b_lo, w_hi[...], w_lo[...], ((0,), (0,)))
-        sp[h, 0:128] = spread[:, 0:128]
-        sp[h, 128:256] = spread[:, 128:256]
+                j = chip(OFFSETS[c][s])
+                cols = pl.ds(pl.multiple_of(128 * j, 128), 128)
+                b_hi, b_lo = split(back[h, pl.ds(2 * j, 2)].reshape(128, 128))
+                spread = spread + dot3(wt_hi[:, cols], wt_lo[:, cols], b_hi, b_lo, ((1,), (0,)))
+        sp[h, 0:128] = spread[0:128].T
+        sp[h, 128:256] = spread[128:256].T
 
         def load_spread(j, i, h=h):
             return sp[h, pl.ds(8 * j + i, 4, stride=64), :]
@@ -631,15 +642,32 @@
         return jnp.sum(total, axis=0, keepdims=True)
 
     rows = [fold(x) for x in (rr, *sums)]
-    part[...] = jnp.concatenate(rows + [jnp.zeros((4, 128), F32)], axis=0)
+    part[...] = jnp.concatenate(rows, axis=0)
     g1 = exchange(lambda p: part, lambda s: gat1.at[s], "gx", gx, r_send.at[0], r_recv.at[0])
     g2 = exchange(lambda p: part2, lambda s: gat2.at[s], "gy", gy, r_send.at[1], r_recv.at[1])
     g1[0]()
     gat1[gx] = part[...]
+    for group in coef_halos:
+        group[2]()
+    for h in range(2):
+        first_halo[h][2]()
+        x1[h][2]()
+        for c in range(4):
+            for s in range(2):
+                peers(c, s, lambda k, peer: o1_copy(h, peer, gx).wait_send())
     g1[1]()
     part2[...] = jnp.sum(gat1[...], axis=0)
     g2[0]()
     gat2[gy] = part2[...]
+    for h in range(2):
+        x2[h][2]()
+        for c in range(4):
+            for s in range(2):
+                peers(c, s, lambda k, peer: o4_copy(h, c, s, k, peer, gx).wait_send())
+    for c in range(4):
+        o2[c][2]()
+        o3[c][2]()
+    g1[2]()
     g2[1]()
     total = jnp.sum(jnp.sum(gat2[...], axis=0), axis=1, keepdims=True)
     norm_now, curvature = total[0:1], total[1:2]
@@ -650,21 +678,6 @@
     scal_ref[...] = jnp.concatenate(
         [jnp.broadcast_to(alpha, (4, 128)), jnp.broadcast_to(beta, (4, 128))], axis=0
     )
-
-    for group in coef_halos:
-        group[2]()
-    for h in range(2):
-        first_halo[h][2]()
-        x1[h][2]()
-        x2[h][2]()
-        for c in range(4):
-            o2[h][c][2]()
-            for s in range(2):
-                peers(c, s, lambda k, peer: o1_copy(h, peer, gx).wait_send())
-                peers(c, s, lambda k, peer: o4_copy(h, c, s, k, peer, gx).wait_send())
-    for c in range(4):
-        o3[c][2]()
-    g1[2]()
     g2[2]()
 
 
@@ -672,16 +685,12 @@
     alpha = scal_ref[0:1, 0:1]
     beta = scal_ref[4:5, 0:1]
 
-    def each(i, carry):
-        v, l = i // 4, i % 4
-        d = dir_ref[v, l]
-        r = res_ref[v, l] - alpha * image_ref[v, l]
-        sol_out[v, l] = sol_ref[v, l] + alpha * d
-        res_out[v, l] = r
-        dir_out[v, l] = r + beta * d
-        return carry
-
-    lax.fori_loop(0, 16, each, 0)
+    for l in range(4):
+        d = dir_ref[0, l]
+        r = res_ref[0, l] - alpha * image_ref[0, l]
+        sol_out[0, l] = sol_ref[0, l] + alpha * d
+        res_out[0, l] = r
+        dir_out[0, l] = r + beta * d
 
 
 def per_device(
@@ -702,6 +711,7 @@
     dma = pltpu.SemaphoreType.DMA
     field = jax.ShapeDtypeStruct((4, 4, 4, 1024), F32)
     in_vmem = pl.BlockSpec(memory_space=pltpu.VMEM)
+    block = pl.BlockSpec((1, 4, 4, 1024), lambda i: (i, 0, 0, 0))
     level = vm((64, 4, 128), F32)
     wide = vm((2, 12, 8, 1024), F32)
     swap_buf = vm((2, N, 16, 128), F32)
@@ -729,6 +739,8 @@
             vm((512, 256), BF16),
             vm((1024, 256), BF16),
             vm((1024, 256), BF16),
+            vm((256, 1024), BF16),
+            vm((256, 1024), BF16),
             vm((256, 256), BF16),
             vm((256, 256), BF16),
             swap_buf,
@@ -736,8 +748,8 @@
             vm((2, 256, 128), F32),
             vm((2, N, 8, 8, 128), F32),
             vm((2, N, 8, 8, 128), F32),
-            vm((2, 8, 2, 4, 2, 8, 128), F32),
-            vm((2, 4, N, 2, 8, 128), F32),
+            vm((8, 2, 4, 2, 2, 8, 128), F32),
+            vm((4, N, 2, 2, 8, 128), F32),
             vm((4, N, 2, 2, 8, 128), F32),
             vm((4, 8, 2, 2, 2, 8, 128), F32),
             vm((4, 2, 2, 2, 8, 8, 128), F32),
@@ -745,18 +757,18 @@
             vm((2, 256, 128), F32),
             swap_buf,
             swap_buf,
-            vm((8, 128), F32),
-            vm((N, 8, 128), F32),
-            vm((8, 128), F32),
-            vm((N, 8, 128), F32),
+            vm((4, 128), F32),
+            vm((N, 4, 128), F32),
+            vm((4, 128), F32),
+            vm((N, 4, 128), F32),
             dma((14,)),
             dma((14,)),
             dma((4, N)),
             dma((4, N)),
             dma((2, N)),
             dma((2, N)),
-            dma((2, 4, N)),
-            dma((2, 4, N)),
+            dma((4, N)),
+            dma((4, N)),
             dma((4, N)),
             dma((4, N)),
             dma((2, N)),
@@ -782,8 +794,9 @@
     return pl.pallas_call(
         update,
         out_shape=(field,) * 3,
-        in_specs=[in_vmem] * 5,
-        out_specs=(in_vmem,) * 3,
+        grid=(4,),
+        in_specs=[block, in_vmem, block, block, block],
+        out_specs=(block,) * 3,
         name="cg_update",
     )(image, scal, direction, solution, residual)
 

time: 127 us -> 118 us (0.929)
  Pallas kernels: 126 us -> 117 us
    pallas_call x1, Pallas kernels: 123 us -> 114 us  [per_device(): pl.pallas_call(kernel, out_shape=(field, jax.ShapeDtypeStruct((8, 128), F...]
where the time goes in v2:
time: 118 us
  Pallas kernels  117 us (99%)
    pallas_call x1, Pallas kernels, per_device(): pl.pallas_call(kernel, out_shape=(field, jax.ShapeDtypeStruct((8, 128), F...  114 us
    pallas_call x1, Pallas kernels, per_device(): pl.pallas_call(update, out_shape=(field,) * 3, grid=(4,), in_specs=[block...  3.36 us

profile of v2, /device:TPU:1, one launch (start us, length us, event | category | flops | bytes accessed | tf_op | source)
XLA Modules:
  0.0 118.1 jit_solution(11450983587413981072)
XLA Ops:
  0.6 114.1 %cg_step.1 = (f32[4,4,4,1024]{3,2,1,0:T(4,128)}, f32[8,128]{1,0:T(8,128)}) custom-call(f32[4,4,4,1024]{3,2,1,0:T(4,128)} %dir_ref.3, f32[4,4,4,1024]{3,2,1,0:T(4,128)} %res_ref.3, f32[4,1024]{1,0:T(4,128)} %north_ref.1, f32[4,1024]{1,0:T(4,128)} %east_ref.1, s32[4,1024]{1,0:T(4,128)} %ocean_ref.1, f32[64,4,64]{2,1,0:T(4,128)} %vert_ref.1, s32[1,512]{1,0:T(1,128)} %bitcast.7, ...), custom_call_target="tpu_custom_call" | custom-call | tf_op jit(solution)/shard_map/cg_step/pallas_call | solution.py:718
  114.7 3.4 %cg_update.1 = (f32[4,4,4,1024]{3,2,1,0:T(4,128)}, f32[4,4,4,1024]{3,2,1,0:T(4,128)}, f32[4,4,4,1024]{3,2,1,0:T(4,128)}) custom-call(f32[4,4,4,1024]{3,2,1,0:T(4,128)} %get-tuple-element.5.image_ref, f32[8,128]{1,0:T(8,128)} %get-tuple-element.6.scal_ref, f32[4,4,4,1024]{3,2,1,0:T(4,128)} %dir_ref.3, f32[4,4,4,1024]{3,2,1,0:T(4,128)} %sol_ref.1, ...), custom_call_target="tpu_custom_call" | custom-call | tf_op jit(solution)/shard_map/cg_update/pallas_call | solution.py:794

commit v3 on v2

--- a/solution.py
+++ b/solution.py
@@ -57,7 +57,7 @@
     return start, wait_recv, wait_send
 
 
-OFFSETS = ((1, -1), (2, -2), (0, 4), (3, -3))
+OFFSETS = ((0, 4), (2, -2), (3, -3), (1, -1))
 
 
 def kernel(
@@ -564,23 +564,26 @@
             if OFFSETS[c][s] == 0:
                 back[h, gx] = u_ref[c, s, core, h]
 
-    def back_chunk(c):
-        return_chunk(c)
-        for h in range(2):
-            send_back(c, h)
-
     forward_chunk(0)
     forward_chunk(1)
     weigh(0)
+    weigh(1)
     forward_chunk(2)
-    weigh(1)
-    back_chunk(0)
+    return_chunk(0)
+    send_back(0, 0)
+    send_back(0, 1)
     forward_chunk(3)
+    return_chunk(1)
+    send_back(1, 0)
+    send_back(1, 1)
     weigh(2)
-    back_chunk(1)
     weigh(3)
-    back_chunk(2)
-    back_chunk(3)
+    return_chunk(2)
+    send_back(2, 0)
+    return_chunk(3)
+    send_back(3, 0)
+    send_back(2, 1)
+    send_back(3, 1)
 
     for h in range(2):
         spread = jnp.zeros((256, 128), F32)
@@ -614,6 +617,7 @@
                 uc[h, 5 + 2 * pair, :, 128 * t : 128 * t + 128] = b
         second_halo[h][0]()
 
+    sums = (zero_tile(), zero_tile(), zero_tile())
     for h in range(2):
         second_halo[h][1]()
         second_halo[h][2]()
@@ -625,15 +629,13 @@
                     k = 4 * v + l
                     image_ref[2 * h + v, l, r : r + 1, :] = tile[k : k + 1]
 
-    def last(i, carry):
-        pq, rq, qq = carry
-        v, l = i // 4, i % 4
-        d, r = dir_ref[v, l], res_ref[v, l]
-        q = d + image_ref[v, l]
-        image_ref[v, l] = q
-        return pq + d * q, rq + r * q, qq + q * q
-
-    sums = lax.fori_loop(0, 16, last, (zero_tile(), zero_tile(), zero_tile()))
+        for i in range(8):
+            pq, rq, qq = sums
+            v, l = 2 * h + i // 4, i % 4
+            d, r = dir_ref[v, l], res_ref[v, l]
+            q = d + image_ref[v, l]
+            image_ref[v, l] = q
+            sums = pq + d * q, rq + r * q, qq + q * q
 
     def fold(x):
         total = x[:, 0:128]
@@ -685,12 +687,13 @@
     alpha = scal_ref[0:1, 0:1]
     beta = scal_ref[4:5, 0:1]
 
-    for l in range(4):
-        d = dir_ref[0, l]
-        r = res_ref[0, l] - alpha * image_ref[0, l]
-        sol_out[0, l] = sol_ref[0, l] + alpha * d
-        res_out[0, l] = r
-        dir_out[0, l] = r + beta * d
+    for v in range(4):
+        for l in range(4):
+            d = dir_ref[v, l]
+            r = res_ref[v, l] - alpha * image_ref[v, l]
+            sol_out[v, l] = sol_ref[v, l] + alpha * d
+            res_out[v, l] = r
+            dir_out[v, l] = r + beta * d
 
 
 def per_device(
@@ -711,7 +714,6 @@
     dma = pltpu.SemaphoreType.DMA
     field = jax.ShapeDtypeStruct((4, 4, 4, 1024), F32)
     in_vmem = pl.BlockSpec(memory_space=pltpu.VMEM)
-    block = pl.BlockSpec((1, 4, 4, 1024), lambda i: (i, 0, 0, 0))
     level = vm((64, 4, 128), F32)
     wide = vm((2, 12, 8, 1024), F32)
     swap_buf = vm((2, N, 16, 128), F32)
@@ -794,9 +796,8 @@
     return pl.pallas_call(
         update,
         out_shape=(field,) * 3,
-        grid=(4,),
-        in_specs=[block, in_vmem, block, block, block],
-        out_specs=(block,) * 3,
+        in_specs=[in_vmem] * 5,
+        out_specs=(in_vmem,) * 3,
         name="cg_update",
     )(image, scal, direction, solution, residual)
 

time: 118 us -> 110 us (0.932)
  Pallas kernels: 117 us -> 109 us
    pallas_call x1, Pallas kernels: 114 us -> 107 us  [per_device(): pl.pallas_call(kernel, out_shape=(field, jax.ShapeDtypeStruct((8, 128), F...]
    pallas_call x1, Pallas kernels: 3.36 us -> 2.13 us  [per_device(): pl.pallas_call(update, out_shape=(field,) * 3, in_specs=[in_vmem] * 5, ou...]
where the time goes in v3:
time: 110 us
  Pallas kernels  109 us (99%)
    pallas_call x1, Pallas kernels, per_device(): pl.pallas_call(kernel, out_shape=(field, jax.ShapeDtypeStruct((8, 128), F...  107 us

profile of v3, /device:TPU:1, one launch (start us, length us, event | category | flops | bytes accessed | tf_op | source)
XLA Modules:
  0.0 109.6 jit_solution(15837100487377259193)
XLA Ops:
  0.6 106.9 %cg_step.1 = (f32[4,4,4,1024]{3,2,1,0:T(4,128)}, f32[8,128]{1,0:T(8,128)}) custom-call(f32[4,4,4,1024]{3,2,1,0:T(4,128)} %dir_ref.3, f32[4,4,4,1024]{3,2,1,0:T(4,128)} %res_ref.3, f32[4,1024]{1,0:T(4,128)} %north_ref.1, f32[4,1024]{1,0:T(4,128)} %east_ref.1, s32[4,1024]{1,0:T(4,128)} %ocean_ref.1, f32[64,4,64]{2,1,0:T(4,128)} %vert_ref.1, s32[1,512]{1,0:T(1,128)} %bitcast.7, ...), custom_call_target="tpu_custom_call" | custom-call | tf_op jit(solution)/shard_map/cg_step/pallas_call | solution.py:720
  107.5 2.1 %cg_update.1 = (f32[4,4,4,1024]{3,2,1,0:T(4,128)}, f32[4,4,4,1024]{3,2,1,0:T(4,128)}, f32[4,4,4,1024]{3,2,1,0:T(4,128)}) custom-call(f32[4,4,4,1024]{3,2,1,0:T(4,128)} %get-tuple-element.5.image_ref, f32[8,128]{1,0:T(8,128)} %get-tuple-element.6.scal_ref, f32[4,4,4,1024]{3,2,1,0:T(4,128)} %dir_ref.3, f32[4,4,4,1024]{3,2,1,0:T(4,128)} %sol_ref.1, ...), custom_call_target="tpu_custom_call" | custom-call | tf_op jit(solution)/shard_map/cg_update/pallas_call | solution.py:796

commit v4 on v3

--- a/solution.py
+++ b/solution.py
@@ -25,6 +25,17 @@
 
 def dot3(a_hi, a_lo, b_hi, b_lo, dims):
     return dot(a_hi, b_hi, dims) + (dot(a_hi, b_lo, dims) + dot(a_lo, b_hi, dims))
+
+
+def far_first(axis, me):
+    if axis == "gx":
+        z, core = me // 2, me % 2
+        chips = [lax.rem(z + off + 8, 8) for off in (4, 3, -3, 2, -2, 1, -1)]
+        return [2 * chip + k for chip in chips for k in range(2)] + [2 * z + 1 - core]
+    y, x = me // 4, me % 4
+    steps = [(dy, dx) for dy in range(4) for dx in range(4) if dy or dx]
+    steps.sort(key=lambda d: -(min(d[0], 4 - d[0]) + min(d[1], 4 - d[1])))
+    return [lax.rem(y + dy, 4) * 4 + lax.rem(x + dx, 4) for dy, dx in steps]
 
 
 def exchange(src, dst, axis, me, send_sem, recv_sem):
@@ -46,7 +57,8 @@
         lax.fori_loop(1, N, body, 0)
 
     def start():
-        each(lambda peer: copy(peer, me).start())
+        for peer in far_first(axis, me):
+            copy(peer, me).start()
 
     def wait_recv():
         each(lambda peer: copy(peer, peer).wait_recv())
@@ -62,18 +74,21 @@
 
 def kernel(
     dir_ref,
-    res_ref,
     north_ref,
     east_ref,
     ocean_ref,
-    vert_ref,
     own_ref,
     row_ref,
     col_ref,
     frac_ref,
-    err_ref,
+    res_any,
+    vert_any,
+    err_any,
     image_ref,
     scal_ref,
+    res_ref,
+    vert_ref,
+    err_ref,
     dt,
     ua,
     ub,
@@ -128,6 +143,7 @@
     o4_recv,
     r_send,
     r_recv,
+    in_sem,
 ):
     gy = lax.axis_index("gy")
     gx = lax.axis_index("gx")
@@ -150,6 +166,15 @@
         return carry
 
     lax.fori_loop(1, N, greet, 0)
+
+    late = [
+        pltpu.make_async_copy(src, dst, in_sem.at[i])
+        for i, (src, dst) in enumerate(
+            ((vert_any, vert_ref), (err_any, err_ref), (res_any, res_ref))
+        )
+    ]
+    for copy in late:
+        copy.start()
 
     for h in range(2):
         for r in range(4):
@@ -206,9 +231,6 @@
         return carry
 
     lax.fori_loop(0, 4, slot_group, 0)
-    hi, lo = split(err_ref[...])
-    e_hi[...] = hi
-    e_lo[...] = lo
 
     pl.semaphore_wait(barrier, 2 * (N - 1))
 
@@ -296,6 +318,12 @@
     hn[1] = north_ref[...]
     he[1] = east_ref[...]
     ho[1] = ocean_ref[...]
+
+    for copy in late:
+        copy.wait()
+    hi, lo = split(err_ref[...])
+    e_hi[...] = hi
+    e_lo[...] = lo
 
     def spread_rows(j, carry):
         for i in range(8):
@@ -720,9 +748,12 @@
     image, scal = pl.pallas_call(
         kernel,
         out_shape=(field, jax.ShapeDtypeStruct((8, 128), F32)),
-        in_specs=[in_vmem] * 11,
+        in_specs=[in_vmem] * 8 + [pl.BlockSpec(memory_space=pl.ANY)] * 3,
         out_specs=(in_vmem,) * 2,
         scratch_shapes=[
+            vm((4, 4, 4, 1024), F32),
+            vm((64, 4, 64), F32),
+            vm((256, 256), F32),
             vm((2, 4, 8, 1024), F32),
             wide,
             wide,
@@ -777,20 +808,21 @@
             dma((2, N)),
             dma((2, N)),
             dma((2, N)),
+            dma((3,)),
         ],
         compiler_params=pltpu.CompilerParams(collective_id=0, has_side_effects=True),
         name="cg_step",
     )(
         direction,
-        residual,
         north_coef,
         east_coef,
         ocean,
-        vert_coef,
         obs_owner.reshape(1, 512),
         obs_row.reshape(1, 512),
         obs_col.reshape(1, 512),
         obs_frac.reshape(2, 512),
+        residual,
+        vert_coef,
         error_inverse.reshape(256, 256),
     )
     return pl.pallas_call(

time: 110 us -> 108 us (0.982)
  Pallas kernels: 109 us -> 107 us
    pallas_call x1, Pallas kernels: 107 us -> 105 us  [per_device(): pl.pallas_call(kernel, out_shape=(field, jax.ShapeDtypeStruct((8, 128), F...]
where the time goes in v4:
time: 108 us; the launch traced here: 107 us
  Pallas kernels  107 us (99%)
    pallas_call x1, Pallas kernels, per_device(): pl.pallas_call(kernel, out_shape=(field, jax.ShapeDtypeStruct((8, 128), F...  105 us

profile of v4, /device:TPU:1, one launch (start us, length us, event | category | flops | bytes accessed | tf_op | source)
XLA Modules:
  0.0 107.4 jit_solution(2939992134768300652)
XLA Ops:
  0.6 104.6 %cg_step.1 = (f32[4,4,4,1024]{3,2,1,0:T(4,128)}, f32[8,128]{1,0:T(8,128)}) custom-call(f32[4,4,4,1024]{3,2,1,0:T(4,128)} %dir_ref.3, f32[4,1024]{1,0:T(4,128)} %north_ref.1, f32[4,1024]{1,0:T(4,128)} %east_ref.1, s32[4,1024]{1,0:T(4,128)} %ocean_ref.1, s32[1,512]{1,0:T(1,128)} %bitcast.7, s32[1,512]{1,0:T(1,128)} %bitcast.8, s32[1,512]{1,0:T(1,128)} %bitcast.9, ...), custom_call_target="tpu_custom_call" | custom-call | tf_op jit(solution)/shard_map/cg_step/pallas_call | solution.py:748
  105.3 2.1 %cg_update.1 = (f32[4,4,4,1024]{3,2,1,0:T(4,128)}, f32[4,4,4,1024]{3,2,1,0:T(4,128)}, f32[4,4,4,1024]{3,2,1,0:T(4,128)}) custom-call(f32[4,4,4,1024]{3,2,1,0:T(4,128)} %get-tuple-element.5.image_ref, f32[8,128]{1,0:T(8,128)} %get-tuple-element.6.scal_ref, f32[4,4,4,1024]{3,2,1,0:T(4,128)} %dir_ref.3, f32[4,4,4,1024]{3,2,1,0:T(4,128)} %sol_ref.1, ...), custom_call_target="tpu_custom_call" | custom-call | tf_op jit(solution)/shard_map/cg_update/pallas_call | solution.py:828

commit v5 on v4

--- a/solution.py
+++ b/solution.py
@@ -150,22 +150,11 @@
 
     barrier = pltpu.get_barrier_semaphore()
 
-    def greet(d, carry):
-        pl.semaphore_signal(
-            barrier,
-            inc=1,
-            device_id={"gx": lax.rem(gx + d, N)},
-            device_id_type=pl.DeviceIdType.MESH,
-        )
-        pl.semaphore_signal(
-            barrier,
-            inc=1,
-            device_id={"gy": lax.rem(gy + d, N)},
-            device_id_type=pl.DeviceIdType.MESH,
-        )
-        return carry
-
-    lax.fori_loop(1, N, greet, 0)
+    for axis, me in (("gx", gx), ("gy", gy)):
+        for peer in far_first(axis, me):
+            pl.semaphore_signal(
+                barrier, inc=1, device_id={axis: peer}, device_id_type=pl.DeviceIdType.MESH
+            )
 
     late = [
         pltpu.make_async_copy(src, dst, in_sem.at[i])
@@ -541,9 +530,11 @@
 
     smoothed_0 = columns(0)
     profile(0, 0, smoothed_0)
+    profile(0, 1, smoothed_0)
     smoothed_1 = columns(1)
     profile(1, 0, smoothed_1)
-    for c in range(1, 4):
+    profile(1, 1, smoothed_1)
+    for c in range(2, 4):
         profile(0, c, smoothed_0)
         profile(1, c, smoothed_1)
     for h in range(2):

time: 108 us -> 108 us (level)
  no operation moved by 1% of the time
where the time goes in v5:
time: 108 us
  Pallas kernels  107 us (99%)
    pallas_call x1, Pallas kernels, per_device(): pl.pallas_call(kernel, out_shape=(field, jax.ShapeDtypeStruct((8, 128), F...  105 us

profile of v5, /device:TPU:1, one launch (start us, length us, event | category | flops | bytes accessed | tf_op | source)
XLA Modules:
  0.0 107.6 jit_solution(9392236108329336658)
XLA Ops:
  0.6 104.9 %cg_step.1 = (f32[4,4,4,1024]{3,2,1,0:T(4,128)}, f32[8,128]{1,0:T(8,128)}) custom-call(f32[4,4,4,1024]{3,2,1,0:T(4,128)} %dir_ref.3, f32[4,1024]{1,0:T(4,128)} %north_ref.1, f32[4,1024]{1,0:T(4,128)} %east_ref.1, s32[4,1024]{1,0:T(4,128)} %ocean_ref.1, s32[1,512]{1,0:T(1,128)} %bitcast.7, s32[1,512]{1,0:T(1,128)} %bitcast.8, s32[1,512]{1,0:T(1,128)} %bitcast.9, ...), custom_call_target="tpu_custom_call" | custom-call | tf_op jit(solution)/shard_map/cg_step/pallas_call | solution.py:739
  105.5 2.1 %cg_update.1 = (f32[4,4,4,1024]{3,2,1,0:T(4,128)}, f32[4,4,4,1024]{3,2,1,0:T(4,128)}, f32[4,4,4,1024]{3,2,1,0:T(4,128)}) custom-call(f32[4,4,4,1024]{3,2,1,0:T(4,128)} %get-tuple-element.5.image_ref, f32[8,128]{1,0:T(8,128)} %get-tuple-element.6.scal_ref, f32[4,4,4,1024]{3,2,1,0:T(4,128)} %dir_ref.3, f32[4,4,4,1024]{3,2,1,0:T(4,128)} %sol_ref.1, ...), custom_call_target="tpu_custom_call" | custom-call | tf_op jit(solution)/shard_map/cg_update/pallas_call | solution.py:819
